TPU v7x, 32 devices: a whole 2x2x4 slice. The times are simulated.
32 devices in a mesh: samples: 4 (over y, x), channel: 4 (over z), spatial: 2 (over core).
Axes of the slice: x: 2, y: 2, z: 4, core: 2. Of those that a mesh axis runs over, the one named last changes fastest.
Arguments:
- features: bfloat16 [512, 4, 2, 1024], P('channel', 'samples', 'spatial'), may hold values from -6 to 6
- conv_one: bfloat16 [27, 512, 512], P(None, 'channel'), may hold values from -0.0625 to 0.0625
- conv_two: bfloat16 [27, 512, 512], P(None, 'channel'), may hold values from -0.0625 to 0.0625
- cotangent: bfloat16 [512, 4, 2, 1024], P('channel', 'samples', 'spatial'), may hold values from -6 to 6
Outputs:
- mixed_out: bfloat16 [512, 4, 2, 1024], P('channel', 'samples', 'spatial')
- input_grad: bfloat16 [512, 4, 2, 1024], P('channel', 'samples', 'spatial')
- grad_one: float32 [27, 512, 512], P(None, 'channel')
- grad_two: float32 [27, 512, 512], P(None, 'channel')
All inputs are finite; a program needn't handle non-finite values.
Results may differ from a plain program's by a relative error of at most 0.017.
Values may be sent and summed in bfloat16 or wider, within the bound.
A program may use at most 128 MiB of HBM per device.

v0:
```python
import jax
import jax.numpy as jnp
from jax import lax
from jax.sharding import PartitionSpec as P

SIDE = 32


def with_halo(shard, sides, width):
    for axis, dim in sides:
        size, length = (lax.axis_size(axis), shard.shape[dim])
        up = [(i, (i + 1) % size) for i in range(size - 1)]
        down = [(j, i) for i, j in up]
        last = lax.slice_in_dim(shard, length - width, length, axis=dim)
        first = lax.slice_in_dim(shard, 0, width, axis=dim)
        before = lax.ppermute(last, axis, up)
        after = lax.ppermute(first, axis, down)
        shard = jnp.concatenate([before, shard, after], axis=dim)
    return shard


def to_grid(values):
    return values.reshape(values.shape[0], values.shape[1], values.shape[2], SIDE, SIDE)


def to_flat(values):
    return values.reshape(values.shape[0], values.shape[1], values.shape[2], SIDE * SIDE)


def as_taps(kernel):
    return kernel.reshape(3, 3, 3, kernel.shape[1], kernel.shape[2])


def forward_conv(source, kernel, rhs_spec):
    return lax.conv_general_dilated(
        source,
        as_taps(kernel),
        (1, 1, 1),
        [(0, 0), (1, 1), (1, 1)],
        dimension_numbers=("CNDHW", rhs_spec, "CNDHW"),
        preferred_element_type=jnp.float32,
    )


def data_grad(source, kernel, rhs_spec):
    flipped = as_taps(kernel)[::-1, ::-1, ::-1]
    return lax.conv_general_dilated(
        source,
        flipped,
        (1, 1, 1),
        [(0, 0), (1, 1), (1, 1)],
        dimension_numbers=("CNDHW", rhs_spec, "CNDHW"),
        preferred_element_type=jnp.float32,
    )


def weight_grad(padded, upstream, out_spec):
    result = lax.conv_general_dilated(
        padded,
        upstream,
        (1, 1, 1),
        [(0, 0), (0, 0), (0, 0)],
        dimension_numbers=("NCDHW", "OIDHW", out_spec),
        preferred_element_type=jnp.float32,
    )
    return result.reshape(27, result.shape[3], result.shape[4])


def pad_plane(values):
    return jnp.pad(values, ((0, 0), (0, 0), (0, 0), (1, 1), (1, 1)))


def body(features, conv_one, conv_two, cotangent):
    rims_x = with_halo(features, (("spatial", 2),), 1)
    whole_x = lax.all_gather(rims_x, "channel", axis=0, tiled=True)
    pre_act = forward_conv(to_grid(whole_x), conv_one, "DHWOI")
    hidden = jax.nn.silu(pre_act).astype(jnp.bfloat16)
    rims_h = with_halo(to_flat(hidden), (("spatial", 2),), 1)
    grid_h = to_grid(rims_h)
    weight_part = conv_two
    mixed_out = lax.psum_scatter(
        to_flat(forward_conv(grid_h, weight_part, "DHWIO")),
        "channel",
        scatter_dimension=0,
        tiled=True,
    ).astype(jnp.bfloat16)
    rims_c = with_halo(cotangent, (("spatial", 2),), 1)
    whole_c = to_grid(lax.all_gather(rims_c, "channel", axis=0, tiled=True))
    hidden_grad = data_grad(whole_c, conv_two, "DHWOI")
    sigmoid_v = jax.nn.sigmoid(pre_act)
    act_grad = (hidden_grad * sigmoid_v * (1.0 + pre_act * (1.0 - sigmoid_v))).astype(jnp.bfloat16)
    rims_g = with_halo(to_flat(act_grad), (("spatial", 2),), 1)
    grid_g = to_grid(rims_g)
    weight_part = conv_one
    input_grad = lax.psum_scatter(
        to_flat(data_grad(grid_g, weight_part, "DHWIO")).astype(jnp.bfloat16),
        "channel",
        scatter_dimension=0,
        tiled=True,
    )
    local_two = weight_grad(pad_plane(grid_h), whole_c[:, :, 1:-1], "DHWNC")
    local_one = weight_grad(pad_plane(to_grid(whole_x)), act_grad, "DHWCN")
    grad_one, grad_two = (
        lax.psum(local_one.astype(jnp.bfloat16), ("samples", "spatial")).astype(jnp.float32),
        lax.psum(local_two.astype(jnp.bfloat16), ("samples", "spatial")).astype(jnp.float32),
    )
    return (mixed_out, input_grad, grad_one, grad_two)


def solution(mesh):
    placed = (
        P("channel", "samples", "spatial", None),
        P(None, "channel", None),
        P(None, "channel", None),
        P("channel", "samples", "spatial", None),
    )
    return jax.shard_map(
        body,
        mesh=mesh,
        in_specs=placed,
        out_specs=(
            P("channel", "samples", "spatial", None),
            P("channel", "samples", "spatial", None),
            P(None, "channel", None),
            P(None, "channel", None),
        ),
        check_vma=False,
    )
```

profile of v0, /device:TPU:0, one launch (start us, length us, event | category | flops | bytes accessed | tf_op | source)
XLA Modules:
  0.0 412.6 jit_solution(8968176364339753036)
XLA Ops:
  7.2 1.9 copy.91
  9.2 2.4 collective-permute-start
  11.6 1.3 collective-permute-start.1
  12.9 2.3 collective-permute-done.1
  15.2 1.9 pad_maximum_fusion.1
  17.2 1.8 copy.106
  19.0 2.0 collective-permute-start.4
  21.1 1.3 collective-permute-start.5
  22.4 2.3 collective-permute-done.5
  24.7 1.9 pad_maximum_fusion.2
  26.7 56.1 %all-gather.3.cloned.1.call-done = bf16[512,1,3,1024]{0,3,2,1:T(8,128)(2,1)} async-done(((bf16[128,1,3,1024]{0,3,2,1:T(8,128)(2,1)}), bf16[512,1,3,1024]{0,3,2,1:T(8,128)(2,1)}) %all-gather.3.cloned.1.call-update) | async-done | bytes 3145744 | tf_op jit(solution)/shard_map/all_gather | solution.py:75
  82.8 3.6 copy.144
  86.4 1.6 fusion.85
  88.0 2.2 copy.96
  90.7 10.3 %multiply_convert_fusion = (bf16[1,32,8,5,128]{4,2,3,1,0:T(8,128)(2,1)S(1)}, f32[1,32,8,5,128]{4,2,3,1,0:T(8,128)}) fusion(bf16[3,3,3,128,512]{4,3,2,1,0:T(8,128)(2,1)S(1)} %bitcast.81, bf16[512,3,32,1,7,2]{0,4,5,2,1,3:T(8,128)(2,1)S(1)} %slice.16, bf16[512,3,32,1,8,5]{0,4,5,2,1,3:T(8,128)(2,1)S(1)} %copy.96, pred[8,5]{0,1:T(8,128)(4,1)S(1)} %copy-done.15), kind=kOutput, calls=%fused_computation.63 | convolution fusion | flops 4452974592 | bytes 9830440 | tf_op jit(solution)/shard_map/conv_general_dilated | solution.py:35
  103.1 1.3 collective-permute-start.3
  104.4 4.6 %collective-permute-start.2 = (bf16[128,1,1,1024]{0,3,2,1:T(8,128)(2,1)}, bf16[128,1,1,1024]{0,3,2,1:T(8,128)(2,1)}, u32[]{:S(2)}, u32[]{:S(2)}) collective-permute-start(bf16[128,1,1,1024]{0,3,2,1:T(8,128)(2,1)} %bitcast.42), channel_id=1, source_target_pairs={{0,1},{2,3},{4,5},{6,7},{8,9},{10,11},{12,13},{14,15},{16,17},{18,... | collective-permute-start | bytes 786440 | tf_op jit(solution)/shard_map/ppermute | solution.py:16
  109.0 1.3 fusion.84
  110.3 3.5 fusion.83
  113.8 32.2 %all-gather.5.cloned.1.call-done = bf16[512,1,3,1024]{0,3,2,1:T(8,128)(2,1)} async-done(((bf16[128,1,3,1024]{0,3,2,1:T(8,128)(2,1)}), bf16[512,1,3,1024]{0,3,2,1:T(8,128)(2,1)}) %all-gather.5.cloned.1.call-update) | async-done | bytes 3145744 | tf_op jit(solution)/shard_map/all_gather | solution.py:88
  145.9 3.6 copy.147
  150.2 2.2 copy.111
  152.9 9.7 %fusion.57 = bf16[1,32,8,5,128]{4,2,3,1,0:T(8,128)(2,1)S(1)} fusion(bf16[3,3,3,128,512]{4,3,2,1,0:T(8,128)(2,1)S(1)} %bitcast.105, bf16[512,3,32,1,7,2]{0,4,5,2,1,3:T(8,128)(2,1)S(1)} %slice.20, bf16[512,3,32,1,8,5]{0,4,5,2,1,3:T(8,128)(2,1)S(1)} %copy.111, f32[1,32,8,5,128]{4,2,3,1,0:T(8,128)S(1)} %copy-done.17, pred[8,5]{0,1:T(8,128)(4,1)S(1)} %copy-done.15), kind=kOutput, calls=%fused_computation.54 | convolution fusion | flops 4453629952 | bytes 9830440 | tf_op jit(solution)/shard_map/conv_general_dilated | solution.py:47
  163.5 2.1 collective-permute-start.6
  165.6 1.3 collective-permute-start.7
  166.9 1.8 copy.140
  168.7 1.8 copy.141
  171.3 2.2 copy.126
  173.6 1.5 fusion.25
  175.1 15.5 %fusion.32 = bf16[3,3,3,128,512,1]{3,4,2,5,1,0:T(8,128)(2,1)} fusion(bf16[512,3,32,8,5,1]{0,3,5,4,2,1:T(8,128)(2,1)S(1)} %get-tuple-element.26, bf16[512,3,32,8,5,1]{0,3,5,4,2,1:T(8,128)(2,1)S(1)} %copy.126, bf16[512,3,32,8,5,1]{0,3,5,4,2,1:T(8,128)(2,1)S(1)} %get-tuple-element.27, bf16[1,32,8,5,128]{4,2,3,1,0:T(8,128)(2,1)S(1)} %fusion.57, ...), kind=kOutput, calls=%fused_computation.36 | convolution fusion | flops 4472799232 | bytes 15663144 | tf_op jit(solution)/shard_map/conv_general_dilated | solution.py:58
  190.5 5.9 %copy.128 = bf16[27,128,512]{2,1,0:T(8,128)(2,1)} copy(bf16[27,128,512]{1,2,0:T(8,128)(2,1)} %bitcast.99) | data formatting | bytes 7077888 | tf_op jit(solution)/shard_map/convert_element_type | solution.py:104
  196.4 2.4 slice.28
  198.8 2.3 copy.100
  201.1 2.3 copy.99
  206.3 4.9 %select_convert_fusion = bf16[1,32,8,5,512]{4,2,3,1,0:T(8,128)(2,1)S(1)} fusion(bf16[3,3,3,128,512]{4,3,2,1,0:T(8,128)(2,1)S(1)} %bitcast.82, bf16[128,3,32,1,7,2]{0,4,5,2,1,3:T(8,128)(2,1)S(1)} %slice.22, bf16[128,3,32,1,8,5]{0,4,5,2,1,3:T(8,128)(2,1)S(1)} %copy.117, pred[8,5]{0,1:T(8,128)(4,1)S(1)} %copy-done.15), kind=kOutput, calls=%fused_computation.34 | convolution fusion | flops 4440915968 | bytes 6176808 | tf_op jit(solution)/shard_map/conv_general_dilated | solution.py:47
  212.3 1.3 copy.134
  213.7 4.4 %pad_maximum_fusion = bf16[128,1,3,32,32]{0,1,4,3,2:T(2,128)(2,1)S(1)} fusion(bf16[128,1,1,32,32]{0,1,4,3,2:T(2,128)(2,1)} %copy.100, bf16[128,1,1,32,32]{0,1,4,3,2:T(2,128)(2,1)S(1)} %bitcast.93, bf16[128,1,1,32,32]{0,1,4,3,2:T(2,128)(2,1)} %copy.99), kind=kLoop, calls=%fused_computation.40 | loop fusion | flops 786432 | bytes 1572864 | tf_op jit(solution)/shard_map/concatenate | solution.py:18
  218.1 20.5 %convolution_convert_fusion = bf16[3,3,3,128,512]{4,3,2,1,0:T(8,128)(2,1)} fusion(bf16[128,1,3,32,32]{0,1,4,3,2:T(2,128)(2,1)S(1)} %pad_maximum_fusion, bf16[512,1,1,32,32]{0,4,3,2,1:T(8,128)(2,1)} %slice.28), kind=kOutput, calls=%fused_computation.35 | convolution fusion | flops 3476226048 | bytes 5373952 | tf_op jit(solution)/shard_map/conv_general_dilated | solution.py:58
  240.9 5.0 %convolution_select_fusion = f32[1,32,8,5,512]{4,2,3,1,0:T(8,128)S(1)} fusion(bf16[3,3,3,128,512]{4,3,2,1,0:T(8,128)(2,1)S(1)} %bitcast.106, bf16[128,3,32,1,7,2]{0,4,5,2,1,3:T(8,128)(2,1)S(1)} %slice.18, bf16[128,3,32,1,8,5]{0,4,5,2,1,3:T(8,128)(2,1)S(1)} %copy.103, pred[8,5]{0,1:T(8,128)(4,1)S(1)} %copy-done.16), kind=kOutput, calls=%fused_computation.39 | convolution fusion | flops 4440260608 | bytes 7487528 | tf_op jit(solution)/shard_map/conv_general_dilated | solution.py:35
  245.9 1.5 copy.104
  247.6 2.6 copy.105
  250.3 1.1 copy.135
  252.2 103.9 %all-reduce.3.cloned.1.call-done = (bf16[27,128,512]{2,1,0:T(8,128)(2,1)}, bf16[27,128,512]{2,1,0:T(8,128)(2,1)}) async-done(((bf16[27,128,512]{2,1,0:T(8,128)(2,1)}, bf16[27,128,512]{2,1,0:T(8,128)(2,1)}), (bf16[27,128,512]{2,1,0:T(8,128)(2,1)}, bf16[27,128,512]{2,1,0:T(8,128)(2,1)})) %all-reduce.3.cloned.1.call-update) | async-done | bytes 7077904 | tf_op jit(solution)/shard_map/psum | solution.py:104
  356.2 6.1 %convert_element_type.52 = f32[27,128,512]{2,1,0:T(8,128)} convert(bf16[27,128,512]{2,1,0:T(8,128)(2,1)} %get-tuple-element.16) | non-fusion elementwise | flops 1769472 | bytes 10616832 | tf_op jit(solution)/shard_map/convert_element_type | solution.py:104
  362.2 4.0 convert_element_type.55
  366.2 35.9 %reduce-scatter.5.cloned.1.call-done = f32[128,1,1,1024]{0,3,2,1:T(8,128)} async-done(((f32[512,1,1,1024]{0,3,2,1:T(8,128)}), f32[128,1,1,1024]{0,3,2,1:T(8,128)}) %reduce-scatter.5.cloned.1.call-update) | async-done | bytes 524304 | tf_op jit(solution)/shard_map/reduce_scatter | solution.py:81
  402.1 1.8 convert_element_type.46
  403.8 1.8 copy.130
  (81 shorter events, 12.6 us)
Async XLA Ops:
  7.2 83.5 %copy-start = (bf16[27,128,512]{2,1,0:T(8,128)(2,1)S(1)}, bf16[27,128,512]{2,1,0:T(8,128)(2,1)}, u32[]{:S(2)}) copy-start(bf16[27,128,512]{2,1,0:T(8,128)(2,1)} %param.5) | copy-start | bytes 10616836
  7.2 75.6 %all-gather.3.cloned.1.call-start = ((), (), s32[]{:S(2)}) async-start(), calls=%async_computation.2 | async-start | bytes 3932160 | tf_op jit(solution)/shard_map/all_gather | solution.py:75
  9.2 3.7 collective-permute-start
  11.6 3.6 collective-permute-start.1
  17.2 128.8 %all-gather.5.cloned.1.call-start = ((), (), s32[]{:S(2)}) async-start(), calls=%async_computation.4 | async-start | bytes 3932160 | tf_op jit(solution)/shard_map/all_gather | solution.py:88
  19.0 3.4 collective-permute-start.4
  21.1 3.6 collective-permute-start.5
  26.6 223.6 %reduce-scatter.7.cloned.1.call-start = ((), (), s32[]{:S(2)}) async-start(), calls=%async_computation.5 | async-start | bytes 1310720
  88.0 22.3 %copy-start.2 = (bf16[512,3,32,1,40]{0,2,4,1,3:T(8,128)(2,1)}, bf16[512,3,32,1,40]{0,2,4,1,3:T(8,128)(2,1)S(1)}, u32[]{:S(2)}) copy-start(bf16[512,3,32,1,40]{0,2,4,1,3:T(8,128)(2,1)S(1)} %get-tuple-element.22) | copy-start | bytes 11796484
  88.0 2.7 copy-start.15
  101.6 0.8 copy-start.6
  103.1 95.7 %collective-permute-start.3 = (bf16[128,1,1,1024]{0,3,2,1:T(8,128)(2,1)}, bf16[128,1,1,1024]{0,3,2,1:T(8,128)(2,1)}, u32[]{:S(2)}, u32[]{:S(2)}) collective-permute-start(bf16[128,1,1,1024]{0,3,2,1:T(8,128)(2,1)} %bitcast.42), channel_id=1, source_target_pairs={{1,0},{3,2},{5,4},{7,6},{9,8},{11,10},{13,12},{15,14},{17,16},{19,... | collective-permute-start | bytes 786440 | tf_op jit(solution)/shard_map/ppermute | solution.py:17
  104.4 96.7 %collective-permute-start.2 = (bf16[128,1,1,1024]{0,3,2,1:T(8,128)(2,1)}, bf16[128,1,1,1024]{0,3,2,1:T(8,128)(2,1)}, u32[]{:S(2)}, u32[]{:S(2)}) collective-permute-start(bf16[128,1,1,1024]{0,3,2,1:T(8,128)(2,1)} %bitcast.42), channel_id=1, source_target_pairs={{0,1},{2,3},{4,5},{6,7},{8,9},{10,11},{12,13},{14,15},{16,17},{18,... | collective-permute-start | bytes 786440 | tf_op jit(solution)/shard_map/ppermute | solution.py:16
  150.2 2.7 copy-start.13
  150.2 2.7 copy-start.17
  152.9 14.1 %copy-start.5 = (bf16[512,3,32,1,8,4]{0,2,5,4,1,3:T(8,128)(2,1)S(1)}, bf16[512,3,32,1,8,4]{0,2,5,4,1,3:T(8,128)(2,1)}, u32[]{:S(2)}) copy-start(bf16[512,3,32,1,8,4]{0,2,5,4,1,3:T(8,128)(2,1)} %get-tuple-element.18) | copy-start | bytes 9437188
  162.7 4.3 %copy-start.11 = (bf16[128,1,1,32,32]{0,3,4,1,2:T(8,128)(2,1)}, bf16[128,1,1,32,32]{0,3,4,1,2:T(8,128)(2,1)S(1)}, u32[]{:S(2)}) copy-start(bf16[128,1,1,32,32]{0,3,4,1,2:T(8,128)(2,1)S(1)} %slice_bitcast_fusion.2) | copy-start | bytes 786436
  162.7 6.0 %copy-start.4 = (bf16[512,3,32,1,8,4]{0,2,5,4,1,3:T(8,128)(2,1)S(1)}, bf16[512,3,32,1,8,4]{0,2,5,4,1,3:T(8,128)(2,1)}, u32[]{:S(2)}) copy-start(bf16[512,3,32,1,8,4]{0,2,5,4,1,3:T(8,128)(2,1)} %get-tuple-element.19) | copy-start | bytes 9437188
  163.5 40.0 %collective-permute-start.6 = (bf16[128,1,1,1024]{0,3,2,1:T(8,128)(2,1)}, bf16[128,1,1,1024]{0,3,2,1:T(8,128)(2,1)}, u32[]{:S(2)}, u32[]{:S(2)}) collective-permute-start(bf16[128,1,1,1024]{0,3,2,1:T(8,128)(2,1)} %bitcast.20), channel_id=1, source_target_pairs={{0,1},{2,3},{4,5},{6,7},{8,9},{10,11},{12,13},{14,15},{16,17},{18,... | collective-permute-start | bytes 786440 | tf_op jit(solution)/shard_map/ppermute | solution.py:16
  165.6 38.9 %collective-permute-start.7 = (bf16[128,1,1,1024]{0,3,2,1:T(8,128)(2,1)}, bf16[128,1,1,1024]{0,3,2,1:T(8,128)(2,1)}, u32[]{:S(2)}, u32[]{:S(2)}) collective-permute-start(bf16[128,1,1,1024]{0,3,2,1:T(8,128)(2,1)} %bitcast.20), channel_id=1, source_target_pairs={{1,0},{3,2},{5,4},{7,6},{9,8},{11,10},{13,12},{15,14},{17,16},{19,... | collective-permute-start | bytes 786440 | tf_op jit(solution)/shard_map/ppermute | solution.py:17
  168.7 1.8 copy-start.10
  168.7 2.2 copy-start.9
  168.7 2.6 copy-start.3
  196.4 9.2 %copy-start.12 = (bf16[128,1,1,32,32]{0,3,4,1,2:T(8,128)(2,1)S(1)}, bf16[128,1,1,32,32]{0,3,4,1,2:T(8,128)(2,1)}, u32[]{:S(2)}) copy-start(bf16[128,1,1,32,32]{0,3,4,1,2:T(8,128)(2,1)} %copy-done.11) | copy-start | bytes 786436
  211.6 2.1 copy-start.7
  213.7 142.5 %all-reduce.3.cloned.1.call-start = ((), (), s32[]{:S(2)}) async-start(), calls=%async_computation.6 | async-start | bytes 14155776 | tf_op jit(solution)/shard_map/psum | solution.py:104
  238.7 163.4 %reduce-scatter.5.cloned.1.call-start = ((), (), s32[]{:S(2)}) async-start(), calls=%async_computation.3 | async-start | bytes 2621440 | tf_op jit(solution)/shard_map/reduce_scatter | solution.py:81
  238.9 2.0 copy-start.14
  238.9 2.0 copy-start.16
  356.2 6.1 %copy-start.8 = (bf16[27,128,512]{2,1,0:T(8,128)(2,1)S(1)}, bf16[27,128,512]{2,1,0:T(8,128)(2,1)}, u32[]{:S(2)}) copy-start(bf16[27,128,512]{2,1,0:T(8,128)(2,1)} %get-tuple-element.17) | copy-start | bytes 10616836
  362.2 43.4 %copy-start.1 = (bf16[27,128,512]{2,1,0:T(8,128)(2,1)S(1)}, bf16[27,128,512]{2,1,0:T(8,128)(2,1)}, u32[]{:S(2)}) copy-start(bf16[27,128,512]{2,1,0:T(8,128)(2,1)} %param.5) | copy-start | bytes 10616836
Sparse Core Ops, SparseCore 0:
  17.3 65.4 all-gather.2
  84.3 61.5 all-gather.4
  213.8 27.3 reduce-scatter.6
  245.0 111.0 all-reduce.2
  358.3 43.7 reduce-scatter.4
where the time goes:
time: 416 us; the launch traced here: 413 us
  waiting for transfers between devices  233 us (56%)
  matrix products  65.8 us (16%)
  local copies, waits for them, and re-layouts  61.1 us (15%)
  other arithmetic  21.6 us (5%)
  starting transfers between devices  16.5 us (4%)
  between operations  14.8 us (4%)
    psum x1, waiting for transfers between devices, body(): lax.psum(local_one.astype(jnp.bfloat16), ('samples', 'spatial'))  104 us
    all_gather x1, waiting for transfers between devices, body(): whole_x = lax.all_gather(rims_x, 'channel', axis=0, tiled=True)  56.1 us
    conv_general_dilated x2, matrix products, weight_grad(): lax.conv_general_dilated(padded, upstream, (1, 1, 1), [(0, 0), (0, 0), (0...  36 us
    reduce_scatter x1, waiting for transfers between devices, body(): lax.psum_scatter(to_flat(forward_conv(grid_h, weight_part, 'DHWIO')), 'ch...  35.9 us
    all_gather x1, waiting for transfers between devices, body(): whole_c = to_grid(lax.all_gather(rims_c, 'channel', axis=0, tiled=True))  32.2 us
    unnamed x52, local copies, waits for them, and re-layouts  24.2 us
    conv_general_dilated x2, matrix products, forward_conv(): lax.conv_general_dilated(source, as_taps(kernel), (1, 1, 1), [(0, 0), (1,...  15.2 us
    conv_general_dilated x2, matrix products, data_grad(): lax.conv_general_dilated(source, flipped, (1, 1, 1), [(0, 0), (1, 1), (1,...  14.6 us
  transfers between devices with their start and end apart: 13, of which 6 were waited for; matrix products, arithmetic and copies ran while one was open for 32% of the time, Pallas kernels for 0%

commit v1 on v0

--- a/solution.py
+++ b/solution.py
@@ -4,6 +4,27 @@
 from jax.sharding import PartitionSpec as P
 
 SIDE = 32
+
+
+def joined_along(parts, dim):
+    parts = jnp.moveaxis(parts, 0, dim)
+    shape = parts.shape
+    return parts.reshape(*shape[:dim], shape[dim] * shape[dim + 1], *shape[dim + 2 :])
+
+
+def grow_blocks(shard, axis):
+    size, index = (lax.axis_size(axis), lax.axis_index(axis))
+    blocks, bit = (shard[None], 1)
+    while bit < size:
+        other = lax.ppermute(blocks, axis, [(i, i ^ bit) for i in range(size)])
+        low = index & bit == 0
+        blocks = jnp.concatenate([jnp.where(low, blocks, other), jnp.where(low, other, blocks)])
+        bit *= 2
+    return blocks
+
+
+def gather_by_bits(x, axis, dim):
+    return joined_along(grow_blocks(x, axis), dim)
 
 
 def with_halo(shard, sides, width):
@@ -85,7 +106,7 @@
         tiled=True,
     ).astype(jnp.bfloat16)
     rims_c = with_halo(cotangent, (("spatial", 2),), 1)
-    whole_c = to_grid(lax.all_gather(rims_c, "channel", axis=0, tiled=True))
+    whole_c = to_grid(gather_by_bits(rims_c, "channel", 0))
     hidden_grad = data_grad(whole_c, conv_two, "DHWOI")
     sigmoid_v = jax.nn.sigmoid(pre_act)
     act_grad = (hidden_grad * sigmoid_v * (1.0 + pre_act * (1.0 - sigmoid_v))).astype(jnp.bfloat16)

time: 416 us -> 506 us (1.22); the launches traced: 413 us -> 497 us
  waiting for transfers between devices: 233 us -> 276 us
  local copies, waits for them, and re-layouts: 61.1 us -> 87.8 us
  other arithmetic: 21.6 us -> 29.2 us
  starting transfers between devices: 16.5 us -> 22.1 us
    ppermute x0 -> x2, waiting for transfers between devices: none -> 132 us  [grow_blocks(): other = lax.ppermute(blocks, axis, [(i, i ^ bit) for i in range(size)])]
    all_gather x1, waiting for transfers between devices: 56.1 us -> 0.01 us  [body(): whole_x = lax.all_gather(rims_x, 'channel', axis=0, tiled=True)]
    all_gather x1 -> x0, waiting for transfers between devices: 32.2 us -> none  [body(): whole_c = to_grid(lax.all_gather(rims_c, 'channel', axis=0, tiled=True))]
    another operation x0 -> x3, local copies, waits for them, and re-layouts: none -> 24.6 us  [to_grid(): values.reshape(values.shape[0], values.shape[1], values.shape[2], SIDE, S...]
    concatenate x0 -> x1, local copies, waits for them, and re-layouts: none -> 5.92 us  [grow_blocks(): jnp.concatenate([jnp.where(low, blocks, other), jnp.where(low, other, blo...]
    ppermute x0 -> x2, starting transfers between devices: none -> 5.24 us  [grow_blocks(): other = lax.ppermute(blocks, axis, [(i, i ^ bit) for i in range(size)])]
    unnamed x52 -> x47, local copies, waits for them, and re-layouts: 24.2 us -> 25.1 us
  transfers between devices with their start and end apart: 13 -> 14, of which waited for: 6 -> 6; matrix products, arithmetic and copies ran while one was open for 32% -> 29% of each run, Pallas kernels for 0% -> 0%
where the time goes in v1:
time: 506 us; the launch traced here: 497 us
  waiting for transfers between devices  276 us (55%)
  local copies, waits for them, and re-layouts  87.8 us (17%)
  matrix products  67.2 us (13%)
  other arithmetic  29.2 us (6%)
  starting transfers between devices  22.1 us (4%)
  between operations  14.5 us (3%)
    ppermute x2, waiting for transfers between devices, grow_blocks(): other = lax.ppermute(blocks, axis, [(i, i ^ bit) for i in range(size)])  132 us
    psum x1, waiting for transfers between devices, body(): lax.psum(local_one.astype(jnp.bfloat16), ('samples', 'spatial'))  104 us
    conv_general_dilated x2, matrix products, weight_grad(): lax.conv_general_dilated(padded, upstream, (1, 1, 1), [(0, 0), (0, 0), (0...  36.5 us
    reduce_scatter x1, waiting for transfers between devices, body(): lax.psum_scatter(to_flat(forward_conv(grid_h, weight_part, 'DHWIO')), 'ch...  35.9 us
    unnamed x47, local copies, waits for them, and re-layouts  25.1 us
    another operation x3, local copies, waits for them, and re-layouts, to_grid(): values.reshape(values.shape[0], values.shape[1], values.shape[2], SIDE, S...  24.6 us
    conv_general_dilated x2, matrix products, data_grad(): lax.conv_general_dilated(source, flipped, (1, 1, 1), [(0, 0), (1, 1), (1,...  16.3 us
    conv_general_dilated x2, matrix products, forward_conv(): lax.conv_general_dilated(source, as_taps(kernel), (1, 1, 1), [(0, 0), (1,...  14.4 us
  transfers between devices with their start and end apart: 14, of which 6 were waited for; matrix products, arithmetic and copies ran while one was open for 29% of the time, Pallas kernels for 0%

profile of v1, /device:TPU:0, one launch (start us, length us, event | category | flops | bytes accessed | tf_op | source)
XLA Modules:
  0.0 497.2 jit_solution(5834561605258486011)
XLA Ops:
  7.2 1.9 copy.89
  9.2 2.4 collective-permute-start
  12.9 2.3 collective-permute-done.1
  15.2 1.9 pad_maximum_fusion.3
  17.2 2.1 collective-permute-start.4
  20.6 2.3 collective-permute-done.5
  22.9 2.0 maximum_bitcast_fusion
  24.9 2.4 collective-permute-start.6
  27.3 42.5 %collective-permute-done.6 = bf16[1,128,1,3,1024]{4,1,3,2,0:T(8,128)(2,1)} collective-permute-done((bf16[1,128,1,3,1024]{4,1,3,2,0:T(8,128)(2,1)}, bf16[1,128,1,3,1024]{4,1,3,2,0:T(8,128)(2,1)}, u32[]{:S(2)}, u32[]{:S(2)}) %collective-permute-start.6) | collective-permute-done | bytes 786464 | tf_op jit(solution)/shard_map/ppermute | solution.py:19
  69.8 1.5 broadcast_select_fusion.3
  73.5 2.8 collective-permute-start.7
  76.4 89.3 %collective-permute-done.7 = bf16[2,128,1,3,1024]{4,1,3,2,0:T(8,128)(2,1)} collective-permute-done((bf16[2,128,1,3,1024]{4,1,3,2,0:T(8,128)(2,1)}, bf16[2,128,1,3,1024]{4,1,3,2,0:T(8,128)(2,1)}, u32[]{:S(2)}, u32[]{:S(2)}) %collective-permute-start.7) | collective-permute-done | bytes 1572896 | tf_op jit(solution)/shard_map/ppermute | solution.py:19
  165.7 2.0 broadcast_select_fusion.1
  167.7 1.9 pad_maximum_fusion
  169.7 5.9 %copy.104 = bf16[4,128,1,3,1024]{1,0,4,3,2:T(4,128)(2,1)} copy(bf16[4,128,1,3,1024]{4,1,3,2,0:T(8,128)(2,1)} %pad_maximum_fusion) | data formatting | bytes 6291456 | tf_op jit(solution)/shard_map/concatenate | solution.py:21
  175.6 5.7 %reshape.112 = bf16[512,3,32,1,32]{0,4,2,1,3:T(8,128)(2,1)} reshape(bf16[4,128,1,3,1024]{1,0,4,3,2:T(4,128)(2,1)} %copy.104) | data formatting | bytes 6291456 | tf_op jit(solution)/shard_map/reshape;reshape | solution.py:44
  181.3 18.4 %reshape_reshape.4 = bf16[512,1,3,32,32]{0,1,4,3,2:T(2,128)(2,1)} reshape(bf16[4,128,1,3,1024]{1,0,4,3,2:T(4,128)(2,1)} %copy.104) | data formatting | bytes 6291456 | tf_op jit(solution)/shard_map/reshape;reshape | solution.py:44
  199.7 3.6 copy.143
  203.9 2.2 copy.107
  206.2 1.9 copy-done.2
  208.1 1.5 slice.20
  209.6 3.6 copy.140
  213.3 1.8 fusion.85
  216.3 2.2 copy.94
  219.0 9.4 %multiply_convert_fusion = (bf16[1,32,8,5,128]{4,2,3,1,0:T(8,128)(2,1)S(1)}, f32[1,32,8,5,128]{4,2,3,1,0:T(8,128)S(1)}) fusion(bf16[3,3,3,128,512]{4,3,2,1,0:T(8,128)(2,1)S(1)} %bitcast.89, bf16[512,3,32,1,7,2]{0,4,5,2,1,3:T(8,128)(2,1)S(1)} %slice.16, bf16[512,3,32,1,8,5]{0,4,5,2,1,3:T(8,128)(2,1)S(1)} %copy.94, pred[8,5]{0,1:T(8,128)(4,1)S(1)} %copy-done.14), kind=kOutput, calls=%fused_computation.69 | convolution fusion | flops 4452974592 | bytes 9830440 | tf_op jit(solution)/shard_map/conv_general_dilated | solution.py:56
  230.6 2.3 collective-permute-start.2
  234.4 11.4 %fusion.57 = bf16[1,32,8,5,128]{4,2,3,1,0:T(8,128)(2,1)S(1)} fusion(bf16[3,3,3,128,512]{4,3,2,1,0:T(8,128)(2,1)} %bitcast.111, bf16[512,3,32,1,7,2]{0,4,5,2,1,3:T(8,128)(2,1)S(1)} %copy-done.10, bf16[512,3,32,1,8,5]{0,4,5,2,1,3:T(8,128)(2,1)S(1)} %copy-done.3, f32[1,32,8,5,128]{4,2,3,1,0:T(8,128)S(1)} %get-tuple-element.29, pred[8,5]{0,1:T(8,128)(4,1)S(1)} %copy-done.14), kind=kOutput, calls=%fused_computation.58 | convolution fusion | flops 4453629952 | bytes 9830440 | tf_op jit(solution)/shard_map/conv_general_dilated | solution.py:68
  246.7 4.4 collective-permute-start.8
  251.1 1.5 collective-permute-start.9
  252.6 1.8 copy.137
  254.4 1.8 copy.138
  256.9 2.2 copy.122
  260.5 15.5 %fusion.32 = bf16[3,3,3,128,512,1]{3,4,2,5,1,0:T(8,128)(2,1)} fusion(bf16[512,3,32,8,5,1]{0,3,5,4,2,1:T(8,128)(2,1)S(1)} %get-tuple-element.30, bf16[512,3,32,8,5,1]{0,3,5,4,2,1:T(8,128)(2,1)S(1)} %copy.122, bf16[512,3,32,8,5,1]{0,3,5,4,2,1:T(8,128)(2,1)S(1)} %get-tuple-element.31, bf16[1,32,8,5,128]{4,2,3,1,0:T(8,128)(2,1)S(1)} %fusion.57, ...), kind=kOutput, calls=%fused_computation.37 | convolution fusion | flops 4472799232 | bytes 15663144 | tf_op jit(solution)/shard_map/conv_general_dilated | solution.py:79
  276.0 6.2 %copy.124 = bf16[27,128,512]{2,1,0:T(8,128)(2,1)} copy(bf16[27,128,512]{1,2,0:T(8,128)(2,1)} %bitcast.105) | data formatting | bytes 7077888 | tf_op jit(solution)/shard_map/convert_element_type | solution.py:125
  282.2 2.3 copy.97
  284.5 2.3 copy.98
  290.6 4.9 select_convert_fusion
  298.0 4.3 pad_maximum_fusion.1
  302.4 21.1 %convolution_convert_fusion = bf16[3,3,3,128,512]{4,3,2,1,0:T(8,128)(2,1)} fusion(bf16[128,1,3,32,32]{0,1,4,3,2:T(2,128)(2,1)S(1)} %pad_maximum_fusion.1, bf16[512,1,3,32,32]{0,1,4,3,2:T(2,128)(2,1)} %reshape_reshape.4), kind=kOutput, calls=%fused_computation.36 | convolution fusion | flops 3476226048 | bytes 6422528 | tf_op jit(solution)/shard_map/conv_general_dilated | solution.py:79
  325.7 5.0 convolution_select_fusion
  330.7 1.5 copy.102
  332.4 2.6 copy.103
  337.1 103.9 %all-reduce.3.cloned.1.call-done = (bf16[27,128,512]{2,1,0:T(8,128)(2,1)}, bf16[27,128,512]{2,1,0:T(8,128)(2,1)}) async-done(((bf16[27,128,512]{2,1,0:T(8,128)(2,1)}, bf16[27,128,512]{2,1,0:T(8,128)(2,1)}), (bf16[27,128,512]{2,1,0:T(8,128)(2,1)}, bf16[27,128,512]{2,1,0:T(8,128)(2,1)})) %all-reduce.3.cloned.1.call-update) | async-done | bytes 7077904 | tf_op jit(solution)/shard_map/psum | solution.py:125
  440.9 6.1 %convert_element_type.52 = f32[27,128,512]{2,1,0:T(8,128)} convert(bf16[27,128,512]{2,1,0:T(8,128)(2,1)} %get-tuple-element.16) | non-fusion elementwise | flops 1769472 | bytes 10616832 | tf_op jit(solution)/shard_map/convert_element_type | solution.py:125
  447.0 4.0 convert_element_type.55
  451.0 35.9 %reduce-scatter.5.cloned.1.call-done = f32[128,1,1,1024]{0,3,2,1:T(8,128)} async-done(((f32[512,1,1,1024]{0,3,2,1:T(8,128)}), f32[128,1,1,1024]{0,3,2,1:T(8,128)}) %reduce-scatter.5.cloned.1.call-update) | async-done | bytes 524304 | tf_op jit(solution)/shard_map/reduce_scatter | solution.py:102
  486.9 1.8 convert_element_type.46
  488.6 1.8 copy.127
  (83 shorter events, 24.3 us)
Async XLA Ops:
  7.2 211.8 %copy-start = (bf16[27,128,512]{2,1,0:T(8,128)(2,1)S(1)}, bf16[27,128,512]{2,1,0:T(8,128)(2,1)}, u32[]{:S(2)}) copy-start(bf16[27,128,512]{2,1,0:T(8,128)(2,1)} %param.5) | copy-start | bytes 10616836
  7.2 202.4 %all-gather.2.cloned.1.call-start = ((), (), s32[]{:S(2)}) async-start(), calls=%async_computation.2 | async-start | bytes 3932160 | tf_op jit(solution)/shard_map/all_gather | solution.py:96
  9.2 3.7 collective-permute-start
  11.6 3.6 collective-permute-start.1
  17.2 317.9 %reduce-scatter.7.cloned.1.call-start = ((), (), s32[]{:S(2)}) async-start(), calls=%async_computation.4 | async-start | bytes 1310720
  17.2 3.4 collective-permute-start.4
  19.3 3.6 collective-permute-start.5
  20.6 2.3 copy-start.11
  22.9 2.0 copy-start.12
  24.9 44.9 %collective-permute-start.6 = (bf16[1,128,1,3,1024]{4,1,3,2,0:T(8,128)(2,1)}, bf16[1,128,1,3,1024]{4,1,3,2,0:T(8,128)(2,1)}, u32[]{:S(2)}, u32[]{:S(2)}) collective-permute-start(bf16[1,128,1,3,1024]{4,1,3,2,0:T(8,128)(2,1)} %maximum_bitcast_fusion), channel_id=1, source_target_pairs={{0,2},{2,0},{4,6},{6,4},{1,3},{3,1},{5,7},{7,5},{8,10},{10,8},{12,... | collective-permute-start | bytes 2359304 | tf_op jit(solution)/shard_map/ppermute | solution.py:19
  71.3 0.9 copy-start.4
  71.3 2.2 copy-start.5
  73.5 92.2 %collective-permute-start.7 = (bf16[2,128,1,3,1024]{4,1,3,2,0:T(8,128)(2,1)}, bf16[2,128,1,3,1024]{4,1,3,2,0:T(8,128)(2,1)}, u32[]{:S(2)}, u32[]{:S(2)}) collective-permute-start(bf16[2,128,1,3,1024]{4,1,3,2,0:T(8,128)(2,1)} %pad_maximum_fusion.2), channel_id=1, source_target_pairs={{0,4},{2,6},{4,0},{6,2},{1,5},{3,7},{5,1},{7,3},{8,12},{10,14},{12... | collective-permute-start | bytes 4718600 | tf_op jit(solution)/shard_map/ppermute | solution.py:19
  206.1 1.9 copy-start.2
  216.3 2.6 copy-start.14
  218.9 15.4 %copy-start.3 = (bf16[512,3,32,1,8,5]{0,4,5,2,1,3:T(8,128)(2,1)S(1)}, bf16[512,3,32,1,8,5]{0,4,5,2,1,3:T(8,128)(2,1)}, u32[]{:S(2)}) copy-start(bf16[512,3,32,1,8,5]{0,4,5,2,1,3:T(8,128)(2,1)} %copy-done.2) | copy-start | bytes 11796484
  218.9 15.4 %copy-start.10 = (bf16[512,3,32,1,7,2]{0,4,5,2,1,3:T(8,128)(2,1)S(1)}, bf16[512,3,32,1,7,2]{0,4,5,2,1,3:T(8,128)(2,1)}, u32[]{:S(2)}) copy-start(bf16[512,3,32,1,7,2]{0,4,5,2,1,3:T(8,128)(2,1)} %slice.20) | copy-start | bytes 4128772
  229.0 0.8 copy-start.6
  230.6 51.6 %collective-permute-start.2 = (bf16[128,1,1,1024]{0,3,2,1:T(8,128)(2,1)}, bf16[128,1,1,1024]{0,3,2,1:T(8,128)(2,1)}, u32[]{:S(2)}, u32[]{:S(2)}) collective-permute-start(bf16[128,1,1,1024]{0,3,2,1:T(8,128)(2,1)} %bitcast.41), channel_id=1, source_target_pairs={{0,1},{2,3},{4,5},{6,7},{8,9},{10,11},{12,13},{14,15},{16,17},{18,... | collective-permute-start | bytes 786440 | tf_op jit(solution)/shard_map/ppermute | solution.py:37
  232.9 51.6 %collective-permute-start.3 = (bf16[128,1,1,1024]{0,3,2,1:T(8,128)(2,1)}, bf16[128,1,1,1024]{0,3,2,1:T(8,128)(2,1)}, u32[]{:S(2)}, u32[]{:S(2)}) collective-permute-start(bf16[128,1,1,1024]{0,3,2,1:T(8,128)(2,1)} %bitcast.41), channel_id=1, source_target_pairs={{1,0},{3,2},{5,4},{7,6},{9,8},{11,10},{13,12},{15,14},{17,16},{19,... | collective-permute-start | bytes 786440 | tf_op jit(solution)/shard_map/ppermute | solution.py:38
  245.9 10.3 %copy-start.9 = (bf16[128,1,1,32,32]{0,3,4,1,2:T(8,128)(2,1)}, bf16[128,1,1,32,32]{0,3,4,1,2:T(8,128)(2,1)S(1)}, u32[]{:S(2)}) copy-start(bf16[128,1,1,32,32]{0,3,4,1,2:T(8,128)(2,1)S(1)} %slice_bitcast_fusion.2) | copy-start | bytes 786436
  246.7 40.1 %collective-permute-start.8 = (bf16[128,1,1,1024]{0,3,2,1:T(8,128)(2,1)}, bf16[128,1,1,1024]{0,3,2,1:T(8,128)(2,1)}, u32[]{:S(2)}, u32[]{:S(2)}) collective-permute-start(bf16[128,1,1,1024]{0,3,2,1:T(8,128)(2,1)} %bitcast.20), channel_id=1, source_target_pairs={{0,1},{2,3},{4,5},{6,7},{8,9},{10,11},{12,13},{14,15},{16,17},{18,... | collective-permute-start | bytes 786440 | tf_op jit(solution)/shard_map/ppermute | solution.py:37
  251.1 36.8 %collective-permute-start.9 = (bf16[128,1,1,1024]{0,3,2,1:T(8,128)(2,1)}, bf16[128,1,1,1024]{0,3,2,1:T(8,128)(2,1)}, u32[]{:S(2)}, u32[]{:S(2)}) collective-permute-start(bf16[128,1,1,1024]{0,3,2,1:T(8,128)(2,1)} %bitcast.20), channel_id=1, source_target_pairs={{1,0},{3,2},{5,4},{7,6},{9,8},{11,10},{13,12},{15,14},{17,16},{19,... | collective-permute-start | bytes 786440 | tf_op jit(solution)/shard_map/ppermute | solution.py:38
  295.9 2.1 copy-start.7
  298.0 143.0 %all-reduce.3.cloned.1.call-start = ((), (), s32[]{:S(2)}) async-start(), calls=%async_computation.5 | async-start | bytes 14155776 | tf_op jit(solution)/shard_map/psum | solution.py:125
  323.5 163.4 %reduce-scatter.5.cloned.1.call-start = ((), (), s32[]{:S(2)}) async-start(), calls=%async_computation.3 | async-start | bytes 2621440 | tf_op jit(solution)/shard_map/reduce_scatter | solution.py:102
  323.7 2.0 copy-start.13
  323.7 2.0 copy-start.15
  440.9 6.1 %copy-start.8 = (bf16[27,128,512]{2,1,0:T(8,128)(2,1)S(1)}, bf16[27,128,512]{2,1,0:T(8,128)(2,1)}, u32[]{:S(2)}) copy-start(bf16[27,128,512]{2,1,0:T(8,128)(2,1)} %get-tuple-element.17) | copy-start | bytes 10616836
  447.0 43.4 %copy-start.1 = (bf16[27,128,512]{2,1,0:T(8,128)(2,1)S(1)}, bf16[27,128,512]{2,1,0:T(8,128)(2,1)}, u32[]{:S(2)}) copy-start(bf16[27,128,512]{2,1,0:T(8,128)(2,1)} %param.5) | copy-start | bytes 10616836
Sparse Core Ops, SparseCore 0:
  17.3 127.1 all-gather.1
  298.1 27.7 reduce-scatter.6
  329.8 111.0 all-reduce.2
  443.1 43.7 reduce-scatter.4
